TPU v7x, 128 devices: a whole 4x4x4 slice. The times are simulated.
128 devices in a mesh: elem: 8 (over y, core), bin: 16 (over z, x).
Axes of the slice: x: 4, y: 4, z: 4, core: 2. Of those that a mesh axis runs over, the one named last changes fastest.
Arguments:
- source: float32 [3, 128, 256, 128], P(None, 'elem', 'bin'), may hold values from -60 to 60
- viscosity: float32 [128, 256, 128], P('elem', 'bin'), may hold values from 0.3 to 3
- coarse_inverse: float32 [8, 128, 128], P('elem', 'bin'), may hold values from -0.06187184 to 2, as said below
- droplets: float32 [7, 8, 65536], P(None, 'elem', 'bin'), may hold values from -3 to 3, as said below
- droplet_elem: int32 [8, 65536], P('elem', 'bin'), may hold values from 0 to 63
- ghost_counts: int32 [2, 8, 16], P(None, 'elem', 'bin'), may hold values from 1 to 8, as said below
- tile_pairs: int32 [2, 8, 4096], P(None, 'elem', 'bin'), may hold values from 0 to 47, as said below
- tile_count: int32 [8, 16], P('elem', 'bin'), may hold values from 32 to 256, as said below
Outputs:
- velocity: float32 [3, 128, 256, 128], P(None, 'elem', 'bin')
- droplet_velocity: float32 [3, 8, 65536], P(None, 'elem', 'bin')
Inputs may be any that keep to these rules, and one draw needn't show every extreme that they name: `ghost_counts`: at least one bin sends 8 blocks to its lower neighbour and one to its upper neighbour. `tile_pairs`: row 0 names own blocks, below 32; row 1 names candidate blocks. `tile_count`: some bin uses all 256 tile slots. `droplets`: positions x, z and y lie in 0 to 1, diameters in 0.5 to 1.5. `coarse_inverse`: diagonal entries lie in 1 to 2.
All inputs are finite; a program needn't handle non-finite values.
Results may differ from a plain program's by a relative error of at most 0.0003.
Values sent between devices are 32-bit elements; how exact they have to be, the bound alone decides.
A program may use at most 128 MiB of HBM per device.

v0:
```python
import jax
import jax.numpy as jnp
import numpy as np
from jax import lax
from jax.sharding import PartitionSpec as P

ITERS = 4
NB = 32
BLOCK = 128
GMAX = 8
TGROUP = 16
PRECISE = lax.Precision.HIGHEST
MASS_TERM = 1.0
RELAXATION = 0.6
COARSE_GAIN = 0.02
SPREAD = 0.1
STIFFNESS = 0.3
TIME_STEP = 0.1


def extended(block, sides, width):
    for axis, dim in sides:
        count = lax.axis_size(axis)
        forward = [(i, i + 1) for i in range(count - 1)]
        forward.append((count - 1, 0))
        backward = [(target, source) for source, target in forward]
        low = lax.ppermute(
            lax.slice_in_dim(block, block.shape[dim] - width, None, axis=dim), axis, forward
        )
        high = lax.ppermute(lax.slice_in_dim(block, 0, width, axis=dim), axis, backward)
        block = jnp.concatenate([low, block, high], axis=dim)
    return block


def legendre_top(points):
    previous = points * 0.0 + 1.0
    current = points * 1.0
    for degree_index in range(1, 7):
        following = ((2 * degree_index + 1) * points * current - degree_index * previous) / (
            degree_index + 1
        )
        previous = current
        current = following
    return current


def gll_tables():
    points = np.array(
        [
            -1.0,
            -0.8717401485096066,
            -0.5917001814331423,
            -0.2092992179024789,
            0.2092992179024789,
            0.5917001814331423,
            0.8717401485096066,
            1.0,
        ]
    )
    weights = np.array(
        [
            0.03571428571428571,
            0.2107042271435061,
            0.3411226924835044,
            0.4124587946587038,
            0.4124587946587038,
            0.3411226924835044,
            0.2107042271435061,
            0.03571428571428571,
        ]
    )
    legendre = legendre_top(points)
    derivative = np.zeros((8, 8))
    for row_index in range(8):
        for col_index in range(8):
            if row_index != col_index:
                derivative[row_index, col_index] = (
                    legendre[row_index]
                    / legendre[col_index]
                    / (points[row_index] - points[col_index])
                )
    derivative[0, 0] = -14.0
    derivative[7, 7] = 14.0
    return (derivative.astype(np.float32), weights.astype(np.float32))


def seam_counts():
    return np.array([2.0, 1.0, 1.0, 1.0, 1.0, 1.0, 1.0, 2.0], np.float32)


def node_line(values, length):
    return jnp.asarray(np.tile(values, length // 8))


def nodal(line_x, line_y, line_z):
    return line_x[:, None, None] * line_y[None, :, None] * line_z[None, None, :]


def along(values, direction, matrix):
    amount = values.shape[direction] // 8
    divided = values.reshape(values.shape[:direction] + (amount, 8) + values.shape[direction + 1 :])
    contracted = jnp.tensordot(divided, matrix, axes=((direction + 1,), (1,)), precision=PRECISE)
    return jnp.moveaxis(contracted, -1, direction + 1).reshape(values.shape)


def seam_pass(values, direction, lower_plane, upper_plane):
    amount = values.shape[direction] // 8
    divided = values.reshape(values.shape[:direction] + (amount, 8) + values.shape[direction + 1 :])
    first_nodes = lax.index_in_dim(divided, 0, direction + 1, keepdims=False)
    last_nodes = lax.index_in_dim(divided, 7, direction + 1, keepdims=False)
    upper_sum = last_nodes + jnp.concatenate(
        [lax.slice_in_dim(first_nodes, 1, amount, axis=direction), upper_plane], direction
    )
    lower_sum = (
        jnp.concatenate(
            [lower_plane, lax.slice_in_dim(last_nodes, 0, amount - 1, axis=direction)], direction
        )
        + first_nodes
    )
    inner = lax.slice_in_dim(divided, 1, 7, axis=direction + 1)
    joined = jnp.concatenate(
        [
            jnp.expand_dims(lower_sum, direction + 1),
            inner,
            jnp.expand_dims(upper_sum, direction + 1),
        ],
        direction + 1,
    )
    return joined.reshape(values.shape)


def assemble(values):
    widened = extended(values, (("elem", 1), ("bin", 2)), 1)
    along_first = seam_pass(widened[:, 1:-1], 1, widened[:, :1], widened[:, -1:])
    along_second = seam_pass(
        along_first[:, :, 1:-1], 2, along_first[:, :, :1], along_first[:, :, -1:]
    )
    return seam_pass(along_second, 3, along_second[:, :, :, -1:], along_second[:, :, :, :1])


def prolong(coarse_cells):
    extent = coarse_cells.shape
    spread_cells = jnp.broadcast_to(
        coarse_cells[:, :, None, :, None, :, None],
        (extent[0], extent[1], 16, extent[2], 16, extent[3], 16),
    )
    return spread_cells.reshape(extent[0], extent[1] * 16, extent[2] * 16, extent[3] * 16)


def tile_force(candidates, own_block, cand_block, active):
    near_rows = candidates[own_block]
    far_rows = candidates[cand_block]
    distance = jnp.zeros((near_rows.shape[0], near_rows.shape[2], far_rows.shape[2]), jnp.float32)
    for component in range(3):
        offset = near_rows[:, component, :, None] - far_rows[:, component, None, :]
        distance = distance + offset * offset
    kernel = jnp.exp(-distance / SPREAD) * far_rows[:, 3, None, :] * active[:, None, None]
    summed = jnp.sum(kernel, axis=2)
    pulled = jnp.einsum("tab,tcb->tca", kernel, far_rows[:, :3], precision=PRECISE)
    return STIFFNESS * near_rows[:, 3, None, :] * (near_rows[:, :3] * summed[:, None, :] - pulled)


def collide_padded(candidates, tile_ids, limit):
    groups = tile_ids.shape[1] // TGROUP
    own_blocks = tile_ids[0].reshape(groups, TGROUP)
    cand_blocks = tile_ids[1].reshape(groups, TGROUP)
    positions = jnp.arange(groups * TGROUP, dtype=jnp.int32).reshape(groups, TGROUP)

    def advance(collision, entries):
        own_block, cand_block, position = entries
        active = (position < limit).astype(jnp.float32)
        return (
            collision.at[own_block].add(tile_force(candidates, own_block, cand_block, active)),
            None,
        )

    start_value = jnp.zeros((NB, 3, candidates.shape[2]), jnp.float32)
    collision, unused = lax.scan(advance, start_value, (own_blocks, cand_blocks, positions))
    return collision


def mask_size(part, kept):
    return jnp.concatenate([part[:3], part[3:] * kept[None, :]], 0)


def shift_height(part, amount):
    return jnp.concatenate([part[:1], part[1:2] + amount, part[2:]], 0)


def body(
    source, viscosity, coarse_inverse, droplets, droplet_elem, ghost_counts, tile_pairs, tile_count
):
    derivative, weights = gll_tables()
    deriv_table = jnp.asarray(derivative)
    square_table = deriv_table * deriv_table
    components, width_x, width_y, width_z = source.shape
    weight = nodal(
        node_line(weights, width_x), node_line(weights, width_y), node_line(weights, width_z)
    )
    multiplicity = nodal(
        node_line(seam_counts(), width_x),
        node_line(seam_counts(), width_y),
        node_line(seam_counts(), width_z),
    )
    coef_w = viscosity * weight
    identity = np.eye(width_z // 8, dtype=np.float32)
    forward_z = jnp.asarray(np.kron(identity, derivative.T))
    backward_z = jnp.asarray(np.kron(identity, derivative))
    square_z = jnp.asarray(np.kron(identity, derivative * derivative))

    def apply_local(component_field):
        summed = MASS_TERM * weight * component_field
        for direction in range(2):
            gradient = along(component_field, direction, deriv_table)
            summed = summed + along(coef_w * gradient, direction, deriv_table.T)
        gradient = jnp.dot(component_field, forward_z, precision=PRECISE)
        return summed + jnp.dot(coef_w * gradient, backward_z, precision=PRECISE)

    diagonal_local = MASS_TERM * weight
    for direction in range(2):
        diagonal_local = diagonal_local + along(coef_w, direction, square_table.T)
    diagonal_local = diagonal_local + jnp.dot(coef_w, square_z, precision=PRECISE)
    diag_sum = assemble(diagonal_local[None])[0]
    forcing = weight * source
    velocity = jnp.zeros_like(source)
    half_x, half_y, half_z = (width_x // 16, width_y // 16, width_z // 16)
    inverse_rows = coarse_inverse[0]
    for sweep_index in range(ITERS):
        if sweep_index == 0:
            residual = assemble(forcing)
        else:
            residual = assemble(
                forcing
                - jnp.stack([apply_local(velocity[component]) for component in range(components)])
            )
        coarse = (
            (weight * residual / multiplicity)
            .reshape(components, half_x, 16, half_y, 16, half_z, 16)
            .sum(axis=(2, 4, 6))
        )
        coarse = coarse.reshape(components, half_x * half_y * half_z)
        partial_dual = jnp.einsum("gh,cg->ch", inverse_rows, coarse, precision=PRECISE)
        coarse_dual = lax.psum(partial_dual, "bin")
        correction = jnp.einsum("gh,ch->cg", inverse_rows, coarse_dual, precision=PRECISE)
        correction = correction.reshape(components, half_x, half_y, half_z)
        velocity = velocity + assemble(
            (RELAXATION * residual / diag_sum + COARSE_GAIN * prolong(correction)) / multiplicity
        )
    element_mean = (weight * velocity).reshape(
        components, width_x // 8, 8, width_y // 8, 8, width_z // 8, 8
    ).sum(axis=(2, 4, 6)) / 8.0
    element_mean = element_mean.reshape(components, -1)
    own_drops = droplets[:, 0]
    position = jnp.stack([own_drops[0], own_drops[1], own_drops[2], own_drops[6]])
    span = GMAX * BLOCK
    block_ids = jnp.arange(span, dtype=jnp.int32) // BLOCK
    lower_count = ghost_counts[0, 0, 0]
    upper_count = ghost_counts[1, 0, 0]
    send_lower = mask_size(position[:, :span], (block_ids < lower_count).astype(jnp.float32))
    send_upper = mask_size(
        position[:, -span:], (block_ids >= GMAX - upper_count).astype(jnp.float32)
    )
    packet = jnp.concatenate([send_lower, send_upper], 1)
    widened = extended(packet, (("bin", 1),), span)
    from_below = shift_height(widened[:, :span], -1.0)
    from_above = shift_height(widened[:, -span:], 1.0)
    candidates = (
        jnp.concatenate([position, from_below, from_above], 1)
        .reshape(4, NB + 2 * GMAX, BLOCK)
        .transpose(1, 0, 2)
    )
    tile_ids = tile_pairs[:, 0]
    limit = tile_count[0, 0]
    collision = collide_padded(candidates, tile_ids, limit)
    collision = collision.transpose(1, 0, 2).reshape(3, own_drops.shape[1])
    element_ids = jnp.arange(element_mean.shape[1], dtype=jnp.int32)
    onehot = (droplet_elem[0][:, None] == element_ids[None, :]).astype(jnp.float32)
    sampled = jnp.einsum("ce,re->cr", element_mean, onehot, precision=PRECISE)
    speeds = own_drops[3:6]
    diameter = own_drops[6]
    updated = speeds + TIME_STEP * ((sampled - speeds) / (diameter * diameter) + collision)
    return (velocity, updated[:, None, :])


def solution(mesh):
    in_specs = (
        P(None, "elem", "bin", None),
        P("elem", "bin", None),
        P("elem", "bin", None),
        P(None, "elem", "bin"),
        P("elem", "bin"),
        P(None, "elem", "bin"),
        P(None, "elem", "bin"),
        P("elem", "bin"),
    )
    out_specs = (P(None, "elem", "bin", None), P(None, "elem", "bin"))
    return jax.shard_map(body, mesh=mesh, in_specs=in_specs, out_specs=out_specs, check_vma=False)
```

profile of v0, /device:TPU:0, one launch (start us, length us, event | category | flops | bytes accessed | tf_op | source)
XLA Modules:
  0.0 924.6 jit_solution(10439911834857078356)
XLA Ops:
  17.4 5.2 collective-permute-start.7
  39.1 5.9 collective-permute-start.3
  74.6 5.9 fusion.32
  80.6 5.3 copy.1461
  86.2 37.4 %psum.28 = f32[3,128]{1,0:T(4,128)S(1)} all-reduce(f32[3,128]{1,0:T(4,128)S(1)} %fusion.112), channel_id=1, replica_groups=mesh['elem'=8,'bin'=16] {'bin'}, use_global_device_ids=true, to_apply=%region_2.0 | all-reduce | flops 384 | bytes 3072 | tf_op jit(solution)/shard_map/psum | solution.py:243
  139.1 5.2 collective-permute-start.11
  237.9 5.4 collective-permute-start.15
  270.4 6.5 fusion.33
  276.9 5.2 copy.1544
  286.2 41.5 %psum.29 = f32[3,128]{1,0:T(4,128)} all-reduce(f32[3,128]{1,0:T(4,128)} %fusion.109), channel_id=1, replica_groups=mesh['elem'=8,'bin'=16] {'bin'}, use_global_device_ids=true, to_apply=%region_5.0 | all-reduce | flops 384 | bytes 3072 | tf_op jit(solution)/shard_map/psum | solution.py:243
  347.2 5.3 collective-permute-start.19
  380.6 4.7 maximum_add_fusion
  451.0 5.3 collective-permute-start.23
  457.0 5.3 collective-permute-start.37
  488.3 6.5 fusion.34
  494.8 5.2 copy.1610
  504.1 37.3 %psum.30 = f32[3,128]{1,0:T(4,128)} all-reduce(f32[3,128]{1,0:T(4,128)} %fusion.106), channel_id=1, replica_groups=mesh['elem'=8,'bin'=16] {'bin'}, use_global_device_ids=true, to_apply=%region_8.0 | all-reduce | flops 384 | bytes 3072 | tf_op jit(solution)/shard_map/psum | solution.py:243
  666.8 5.3 collective-permute-start.31
  696.0 6.0 fusion.35
  702.0 5.3 copy.1676
  707.5 40.4 %psum.31 = f32[3,128]{1,0:T(4,128)S(1)} all-reduce(f32[3,128]{1,0:T(4,128)S(1)} %fusion.103), channel_id=1, replica_groups=mesh['elem'=8,'bin'=16] {'bin'}, use_global_device_ids=true, to_apply=%region_11.12 | all-reduce | flops 384 | bytes 3072 | tf_op jit(solution)/shard_map/psum | solution.py:243
  759.3 5.3 collective-permute-start.35
  764.6 133.8 %while.10 = (s32[]{:T(128)}, f32[32,3,128]{2,1,0:T(4,128)S(1)}, s32[16,16]{1,0:T(8,128)}, f32[48,4,128]{2,1,0:T(4,128)S(1)}, s32[16,16]{1,0:T(8,128)}, /*index=5*/s32[16,16]{1,0:T(8,128)}, s32[]{:T(128)}, s32[]{:T(128)}) while((s32[]{:T(128)}, f32[32,3,128]{2,1,0:T(4,128)S(1)}, s32[16,16]{1,0:T(8,128)}, f32[48,4,128]{2,1,0:T(4,128)S(1)}, ...), condition=%wide.region_17.18_spmd, body=%wide.region_14.17_spmd.sunk | while | flops 16017570 | bytes 566241 | solution.py:178
  912.4 6.3 multiply_reduce_fusion
  (854 shorter events, 656.9 us)
Async XLA Ops:
  5.6 10.2 %collective-permute-start.4 = (f32[1,1,16,128]{3,2,1,0:T(8,128)S(1)}, f32[1,1,16,128]{3,2,1,0:T(8,128)S(1)}, u32[]{:S(2)}, u32[]{:S(2)}) collective-permute-start(f32[1,1,16,128]{3,2,1,0:T(8,128)S(1)} %get-tuple-element.284), channel_id=1, source_target_pairs={{0,16},{16,32},{32,48},{48,64},{64,80},{80,96},{96,112},{112,0},{1... | collective-permute-start | bytes 24584 | tf_op jit(solution)/shard_map/ppermute | solution.py:27
  5.6 10.2 %collective-permute-start.5 = (f32[1,1,16,128]{3,2,1,0:T(8,128)S(1)}, f32[1,1,16,128]{3,2,1,0:T(8,128)S(1)}, u32[]{:S(2)}, u32[]{:S(2)}) collective-permute-start(f32[1,1,16,128]{3,2,1,0:T(8,128)S(1)} %get-tuple-element.285), channel_id=1, source_target_pairs={{16,0},{32,16},{48,32},{64,48},{80,64},{96,80},{112,96},{0,112},{1... | collective-permute-start | bytes 24584 | tf_op jit(solution)/shard_map/ppermute | solution.py:30
  10.2 27.7 %collective-permute-start = (f32[3,1,16,128]{3,2,1,0:T(8,128)}, f32[3,1,16,128]{3,2,1,0:T(8,128)}, u32[]{:S(2)}, u32[]{:S(2)}) collective-permute-start(f32[3,1,16,128]{3,2,1,0:T(8,128)} %get-tuple-element.259), channel_id=1, source_target_pairs={{0,16},{16,32},{32,48},{48,64},{64,80},{80,96},{96,112},{112,0},{1... | collective-permute-start | bytes 73736 | tf_op jit(solution)/shard_map/ppermute | solution.py:27
  10.2 27.7 %collective-permute-start.1 = (f32[3,1,16,128]{3,2,1,0:T(8,128)}, f32[3,1,16,128]{3,2,1,0:T(8,128)}, u32[]{:S(2)}, u32[]{:S(2)}) collective-permute-start(f32[3,1,16,128]{3,2,1,0:T(8,128)} %get-tuple-element.260), channel_id=1, source_target_pairs={{16,0},{32,16},{48,32},{64,48},{80,64},{96,80},{112,96},{0,112},{1... | collective-permute-start | bytes 73736 | tf_op jit(solution)/shard_map/ppermute | solution.py:30
  15.8 8.1 collective-permute-start.6
  39.1 11.4 %collective-permute-start.2 = (f32[3,18,1,128]{3,2,1,0:T(1,128)S(1)}, f32[3,18,1,128]{3,2,1,0:T(1,128)S(1)}, u32[]{:S(2)}, u32[]{:S(2)}) collective-permute-start(f32[3,18,1,128]{3,2,1,0:T(1,128)S(1)} %get-tuple-element.213), channel_id=1, source_target_pairs={{0,1},{1,2},{2,3},{3,4},{4,5},{5,6},{6,7},{7,8},{8,9},{9,10},{10,1... | collective-permute-start | bytes 82952 | tf_op jit(solution)/shard_map/ppermute | solution.py:27
  39.1 11.3 %collective-permute-start.3 = (f32[3,18,1,128]{3,2,1,0:T(1,128)S(1)}, f32[3,18,1,128]{3,2,1,0:T(1,128)S(1)}, u32[]{:S(2)}, u32[]{:S(2)}) collective-permute-start(f32[3,18,1,128]{3,2,1,0:T(1,128)S(1)} %get-tuple-element.214), channel_id=1, source_target_pairs={{1,0},{2,1},{3,2},{4,3},{5,4},{6,5},{7,6},{8,7},{9,8},{10,9},{11,1... | collective-permute-start | bytes 82952 | tf_op jit(solution)/shard_map/ppermute | solution.py:30
  129.2 7.6 collective-permute-start.9
  139.0 7.2 collective-permute-start.10
  237.8 7.2 collective-permute-start.14
  336.1 8.3 collective-permute-start.17
  347.1 7.5 collective-permute-start.18
  347.2 7.4 collective-permute-start.19
  450.9 11.4 %collective-permute-start.22 = (f32[3,18,1,128]{3,2,1,0:T(1,128)S(1)}, f32[3,18,1,128]{3,2,1,0:T(1,128)S(1)}, u32[]{:S(2)}, u32[]{:S(2)}) collective-permute-start(f32[3,18,1,128]{3,2,1,0:T(1,128)S(1)} %get-tuple-element.201), channel_id=1, source_target_pairs={{0,1},{1,2},{2,3},{3,4},{4,5},{5,6},{6,7},{7,8},{8,9},{9,10},{10,1... | collective-permute-start | bytes 82952 | tf_op jit(solution)/shard_map/ppermute | solution.py:27
  451.0 11.3 %collective-permute-start.23 = (f32[3,18,1,128]{3,2,1,0:T(1,128)S(1)}, f32[3,18,1,128]{3,2,1,0:T(1,128)S(1)}, u32[]{:S(2)}, u32[]{:S(2)}) collective-permute-start(f32[3,18,1,128]{3,2,1,0:T(1,128)S(1)} %get-tuple-element.202), channel_id=1, source_target_pairs={{1,0},{2,1},{3,2},{4,3},{5,4},{6,5},{7,6},{8,7},{9,8},{10,9},{11,1... | collective-permute-start | bytes 82952 | tf_op jit(solution)/shard_map/ppermute | solution.py:30
  457.0 208.2 %collective-permute-start.36 = (f32[4,1024]{1,0:T(4,128)}, f32[4,1024]{1,0:T(4,128)}, u32[]{:S(2)}, u32[]{:S(2)}) collective-permute-start(f32[4,1024]{1,0:T(4,128)} %get-tuple-element.291), channel_id=1, source_target_pairs={{0,1},{1,2},{2,3},{3,4},{4,5},{5,6},{6,7},{7,8},{8,9},{9,10},{10,1... | collective-permute-start | bytes 49160 | tf_op jit(solution)/shard_map/ppermute | solution.py:27
  457.0 215.1 %collective-permute-start.37 = (f32[4,1024]{1,0:T(4,128)}, f32[4,1024]{1,0:T(4,128)}, u32[]{:S(2)}, u32[]{:S(2)}) collective-permute-start(f32[4,1024]{1,0:T(4,128)} %get-tuple-element.292), channel_id=1, source_target_pairs={{1,0},{2,1},{3,2},{4,3},{5,4},{6,5},{7,6},{8,7},{9,8},{10,9},{11,1... | collective-permute-start | bytes 49160 | tf_op jit(solution)/shard_map/ppermute | solution.py:30
  549.7 8.3 collective-permute-start.25
  561.3 8.6 collective-permute-start.26
  562.1 7.8 collective-permute-start.27
  666.7 7.7 collective-permute-start.30
  666.8 7.6 collective-permute-start.31
  759.2 139.2 %collective-permute-start.34 = (f32[3,18,1,128]{3,2,1,0:T(1,128)S(1)}, f32[3,18,1,128]{3,2,1,0:T(1,128)S(1)}, u32[]{:S(2)}, u32[]{:S(2)}) collective-permute-start(f32[3,18,1,128]{3,2,1,0:T(1,128)S(1)} %get-tuple-element.193), channel_id=1, source_target_pairs={{0,1},{1,2},{2,3},{3,4},{4,5},{5,6},{6,7},{7,8},{8,9},{9,10},{10,1... | collective-permute-start | bytes 82952 | tf_op jit(solution)/shard_map/ppermute | solution.py:27
  759.3 139.1 %collective-permute-start.35 = (f32[3,18,1,128]{3,2,1,0:T(1,128)S(1)}, f32[3,18,1,128]{3,2,1,0:T(1,128)S(1)}, u32[]{:S(2)}, u32[]{:S(2)}) collective-permute-start(f32[3,18,1,128]{3,2,1,0:T(1,128)S(1)} %get-tuple-element.194), channel_id=1, source_target_pairs={{1,0},{2,1},{3,2},{4,3},{5,4},{6,5},{7,6},{8,7},{9,8},{10,9},{11,1... | collective-permute-start | bytes 82952 | tf_op jit(solution)/shard_map/ppermute | solution.py:30
  (63 other events, 532.1 us)
where the time goes:
time: 935 us; the launch traced here: 925 us
  local copies, waits for them, and re-layouts  342 us (37%)
  other arithmetic  209 us (22%)
  blocking collectives  157 us (17%)
  matrix products  120 us (13%)
  starting transfers between devices  82.7 us (9%)
    psum x4, blocking collectives, body(): coarse_dual = lax.psum(partial_dual, 'bin')  157 us
    ppermute x19, starting transfers between devices, extended(): lax.ppermute(lax.slice_in_dim(block, 0, width, axis=dim), axis, backward)  79.5 us
    dot_general x38, matrix products, along(): jnp.tensordot(divided, matrix, axes=((direction + 1,), (1,)), precision=P...  48.1 us
    dot_general x16, matrix products, tile_force(): jnp.einsum('tab,tcb->tca', kernel, far_rows[:, :3], precision=PRECISE)  41.6 us
    another operation x18, local copies, waits for them, and re-layouts, along(): values.reshape(values.shape[:direction] + (amount, 8) + values.shape[dire...  38.6 us
    slice x27, local copies, waits for them, and re-layouts, seam_pass(): inner = lax.slice_in_dim(divided, 1, 7, axis=direction + 1)  35.8 us
    concatenate x16, local copies, waits for them, and re-layouts, seam_pass(): jnp.concatenate([jnp.expand_dims(lower_sum, direction + 1), inner, jnp.ex...  33 us
    slice x10, other arithmetic, seam_pass(): last_nodes = lax.index_in_dim(divided, 7, direction + 1, keepdims=False)  29.1 us
  transfers between devices with their start and end apart: 38, of which 10 were waited for; matrix products, arithmetic and copies ran while one was open for 35% of the time, Pallas kernels for 0%

commit v1 on v0

--- a/solution.py
+++ b/solution.py
@@ -1,3 +1,4 @@
+import functools
 import jax
 import jax.numpy as jnp
 import numpy as np
@@ -16,6 +17,19 @@
 SPREAD = 0.1
 STIFFNESS = 0.3
 TIME_STEP = 0.1
+
+
+def fix_corner(payload, shard_axis):
+    shares = lax.axis_size(shard_axis)
+    x_next, y1 = (payload, 0)
+    while 1 << y1 < shares:
+        big = lax.ppermute(x_next, shard_axis, tuple(((b, b ^ 1 << y1) for b in range(shares))))
+        x_next = x_next + big
+        y1 = y1 + 1
+    return x_next
+
+
+spans_change = functools.partial(fix_corner, shard_axis="bin")
 
 
 def extended(block, sides, width):
@@ -240,7 +254,7 @@
         )
         coarse = coarse.reshape(components, half_x * half_y * half_z)
         partial_dual = jnp.einsum("gh,cg->ch", inverse_rows, coarse, precision=PRECISE)
-        coarse_dual = lax.psum(partial_dual, "bin")
+        coarse_dual = spans_change(partial_dual)
         correction = jnp.einsum("gh,ch->cg", inverse_rows, coarse_dual, precision=PRECISE)
         correction = correction.reshape(components, half_x, half_y, half_z)
         velocity = velocity + assemble(

time: 935 us -> 823 us (0.88)
  blocking collectives: 157 us -> 0 us
  waiting for transfers between devices: 8.91 us -> 54.7 us
  other arithmetic: 209 us -> 186 us
  starting transfers between devices: 82.7 us -> 101 us
    psum x4 -> x0, blocking collectives: 157 us -> none  [body(): coarse_dual = lax.psum(partial_dual, 'bin')]
    ppermute x0 -> x16, waiting for transfers between devices: none -> 40.8 us  [fix_corner(): lax.ppermute(x_next, shard_axis, tuple(((b, b ^ 1 << y1) for b in range(s...]
    ppermute x0 -> x16, starting transfers between devices: none -> 18.1 us  [fix_corner(): lax.ppermute(x_next, shard_axis, tuple(((b, b ^ 1 << y1) for b in range(s...]
    select_n x16, other arithmetic: 11 us -> 0.2 us  [tile_force(): near_rows = candidates[own_block]]
    convert_element_type x16, other arithmetic: 21.3 us -> 10.5 us  [advance(): active = (position < limit).astype(jnp.float32)]
    unnamed x117 -> x119, local copies, waits for them, and re-layouts: 26.7 us -> 26.7 us
  transfers between devices with their start and end apart: 38 -> 54, of which waited for: 10 -> 24; matrix products, arithmetic and copies ran while one was open for 35% -> 25% of each run, Pallas kernels for 0% -> 0%
where the time goes in v1:
time: 823 us; the launch traced here: 809 us
  local copies, waits for them, and re-layouts  342 us (42%)
  other arithmetic  186 us (23%)
  matrix products  119 us (14%)
  starting transfers between devices  101 us (12%)
  waiting for transfers between devices  54.7 us (7%)
    ppermute x19, starting transfers between devices, extended(): lax.ppermute(lax.slice_in_dim(block, 0, width, axis=dim), axis, backward)  76.5 us
    dot_general x38, matrix products, along(): jnp.tensordot(divided, matrix, axes=((direction + 1,), (1,)), precision=P...  48.2 us
    dot_general x16, matrix products, tile_force(): jnp.einsum('tab,tcb->tca', kernel, far_rows[:, :3], precision=PRECISE)  41.6 us
    ppermute x16, waiting for transfers between devices, fix_corner(): lax.ppermute(x_next, shard_axis, tuple(((b, b ^ 1 << y1) for b in range(s...  40.8 us
    another operation x18, local copies, waits for them, and re-layouts, along(): values.reshape(values.shape[:direction] + (amount, 8) + values.shape[dire...  38.7 us
    slice x27, local copies, waits for them, and re-layouts, seam_pass(): inner = lax.slice_in_dim(divided, 1, 7, axis=direction + 1)  35.8 us
    concatenate x16, local copies, waits for them, and re-layouts, seam_pass(): jnp.concatenate([jnp.expand_dims(lower_sum, direction + 1), inner, jnp.ex...  32.8 us
    slice x10, other arithmetic, seam_pass(): last_nodes = lax.index_in_dim(divided, 7, direction + 1, keepdims=False)  29.1 us
  transfers between devices with their start and end apart: 54, of which 24 were waited for; matrix products, arithmetic and copies ran while one was open for 25% of the time, Pallas kernels for 0%

profile of v1, /device:TPU:0, one launch (start us, length us, event | category | flops | bytes accessed | tf_op | source)
XLA Modules:
  0.0 808.7 jit_solution(1076017220118450317)
XLA Ops:
  17.5 5.2 collective-permute-start.7
  31.1 5.6 collective-permute-start.3
  50.6 4.3 slice.1187
  66.4 5.9 fusion.32
  86.9 14.0 %collective-permute-start.11 = (f32[3,128]{1,0:T(4,128)S(1)}, f32[3,128]{1,0:T(4,128)S(1)}, u32[]{:S(2)}, u32[]{:S(2)}) collective-permute-start(f32[3,128]{1,0:T(4,128)S(1)} %add.487), channel_id=1, source_target_pairs={{0,8},{1,9},{2,10},{3,11},{4,12},{5,13},{6,14},{7,15},{8,0},{9,1},... | collective-permute-start | bytes 4616 | tf_op jit(solution)/shard_map/ppermute | solution.py:26
  106.4 5.3 copy.1461
  127.9 4.6 collective-permute-start.15
  226.0 5.4 collective-permute-start.19
  241.8 4.3 slice.1259
  258.6 6.5 fusion.33
  272.3 5.0 collective-permute-done.21
  282.8 5.2 copy.1544
  340.5 4.7 maximum_add_fusion
  411.0 5.3 collective-permute-start.31
  443.9 6.5 fusion.34
  468.2 5.3 copy.1610
  596.5 5.3 collective-permute-start.43
  602.0 5.3 collective-permute-start.53
  628.9 6.0 fusion.35
  639.0 4.9 collective-permute-done.45
  647.5 5.4 copy.1676
  664.4 5.3 collective-permute-start.51
  669.7 112.7 %while.10 = (s32[]{:T(128)}, f32[32,3,128]{2,1,0:T(4,128)S(1)}, s32[16,16]{1,0:T(8,128)S(1)}, f32[48,4,128]{2,1,0:T(4,128)S(1)}, s32[16,16]{1,0:T(8,128)S(1)}, /*index=5*/s32[16,16]{1,0:T(8,128)S(1)}, s32[]{:T(128)}, s32[]{:T(128)}) while((s32[]{:T(128)}, f32[32,3,128]{2,1,0:T(4,128)S(1)}, s32[16,16]{1,0:T(8,128)S(1)}, ...), condition=%wide.region_13.14_spmd, body=%wide.region_10.13_spmd.sunk | while | flops 16017570 | bytes 566241 | solution.py:192
  796.4 6.3 multiply_reduce_fusion
  (896 shorter events, 670.5 us)
Async XLA Ops:
  5.5 10.2 %collective-permute-start.4 = (f32[1,1,16,128]{3,2,1,0:T(8,128)S(1)}, f32[1,1,16,128]{3,2,1,0:T(8,128)S(1)}, u32[]{:S(2)}, u32[]{:S(2)}) collective-permute-start(f32[1,1,16,128]{3,2,1,0:T(8,128)S(1)} %get-tuple-element.284), channel_id=1, source_target_pairs={{0,16},{16,32},{32,48},{48,64},{64,80},{80,96},{96,112},{112,0},{1... | collective-permute-start | bytes 24584 | tf_op jit(solution)/shard_map/ppermute | solution.py:41
  5.6 10.2 %collective-permute-start.5 = (f32[1,1,16,128]{3,2,1,0:T(8,128)S(1)}, f32[1,1,16,128]{3,2,1,0:T(8,128)S(1)}, u32[]{:S(2)}, u32[]{:S(2)}) collective-permute-start(f32[1,1,16,128]{3,2,1,0:T(8,128)S(1)} %get-tuple-element.285), channel_id=1, source_target_pairs={{16,0},{32,16},{48,32},{64,48},{80,64},{96,80},{112,96},{0,112},{1... | collective-permute-start | bytes 24584 | tf_op jit(solution)/shard_map/ppermute | solution.py:44
  10.2 19.1 %collective-permute-start = (f32[3,1,16,128]{3,2,1,0:T(8,128)}, f32[3,1,16,128]{3,2,1,0:T(8,128)}, u32[]{:S(2)}, u32[]{:S(2)}) collective-permute-start(f32[3,1,16,128]{3,2,1,0:T(8,128)} %get-tuple-element.259), channel_id=1, source_target_pairs={{0,16},{16,32},{32,48},{48,64},{64,80},{80,96},{96,112},{112,0},{1... | collective-permute-start | bytes 73736 | tf_op jit(solution)/shard_map/ppermute | solution.py:41
  10.2 19.1 %collective-permute-start.1 = (f32[3,1,16,128]{3,2,1,0:T(8,128)}, f32[3,1,16,128]{3,2,1,0:T(8,128)}, u32[]{:S(2)}, u32[]{:S(2)}) collective-permute-start(f32[3,1,16,128]{3,2,1,0:T(8,128)} %get-tuple-element.260), channel_id=1, source_target_pairs={{16,0},{32,16},{48,32},{64,48},{80,64},{96,80},{112,96},{0,112},{1... | collective-permute-start | bytes 73736 | tf_op jit(solution)/shard_map/ppermute | solution.py:44
  15.8 8.1 collective-permute-start.6
  31.1 9.7 %collective-permute-start.2 = (f32[3,18,1,128]{3,2,1,0:T(1,128)}, f32[3,18,1,128]{3,2,1,0:T(1,128)}, u32[]{:S(2)}, u32[]{:S(2)}) collective-permute-start(f32[3,18,1,128]{3,2,1,0:T(1,128)} %get-tuple-element.213), channel_id=1, source_target_pairs={{0,1},{1,2},{2,3},{3,4},{4,5},{5,6},{6,7},{7,8},{8,9},{9,10},{10,1... | collective-permute-start | bytes 82952 | tf_op jit(solution)/shard_map/ppermute | solution.py:41
  31.1 9.7 %collective-permute-start.3 = (f32[3,18,1,128]{3,2,1,0:T(1,128)}, f32[3,18,1,128]{3,2,1,0:T(1,128)}, u32[]{:S(2)}, u32[]{:S(2)}) collective-permute-start(f32[3,18,1,128]{3,2,1,0:T(1,128)} %get-tuple-element.214), channel_id=1, source_target_pairs={{1,0},{2,1},{3,2},{4,3},{5,4},{6,5},{7,6},{8,7},{9,8},{10,9},{11,1... | collective-permute-start | bytes 82952 | tf_op jit(solution)/shard_map/ppermute | solution.py:44
  86.9 24.7 %collective-permute-start.11 = (f32[3,128]{1,0:T(4,128)S(1)}, f32[3,128]{1,0:T(4,128)S(1)}, u32[]{:S(2)}, u32[]{:S(2)}) collective-permute-start(f32[3,128]{1,0:T(4,128)S(1)} %add.487), channel_id=1, source_target_pairs={{0,8},{1,9},{2,10},{3,11},{4,12},{5,13},{6,14},{7,15},{8,0},{9,1},... | collective-permute-start | bytes 4616 | tf_op jit(solution)/shard_map/ppermute | solution.py:26
  117.3 7.6 collective-permute-start.13
  127.1 7.2 collective-permute-start.14
  225.9 7.3 collective-permute-start.18
  226.0 7.2 collective-permute-start.19
  296.3 8.2 %collective-permute-start.25 = (f32[3,1,16,128]{2,3,1,0:T(8,128)}, f32[3,1,16,128]{2,3,1,0:T(8,128)}, u32[]{:S(2)}, u32[]{:S(2)}) collective-permute-start(f32[3,1,16,128]{2,3,1,0:T(8,128)} %get-tuple-element.118), channel_id=1, source_target_pairs={{16,0},{32,16},{48,32},{64,48},{80,64},{96,80},{112,96},{0,112},{1... | collective-permute-start | bytes 73736 | tf_op jit(solution)/shard_map/ppermute | solution.py:44
  307.3 7.2 collective-permute-start.26
  410.8 7.2 collective-permute-start.30
  411.0 7.0 collective-permute-start.31
  481.8 8.3 %collective-permute-start.37 = (f32[3,1,16,128]{2,3,1,0:T(8,128)}, f32[3,1,16,128]{2,3,1,0:T(8,128)}, u32[]{:S(2)}, u32[]{:S(2)}) collective-permute-start(f32[3,1,16,128]{2,3,1,0:T(8,128)} %get-tuple-element.106), channel_id=1, source_target_pairs={{16,0},{32,16},{48,32},{64,48},{80,64},{96,80},{112,96},{0,112},{1... | collective-permute-start | bytes 73736 | tf_op jit(solution)/shard_map/ppermute | solution.py:44
  492.9 7.5 collective-permute-start.38
  596.5 10.9 %collective-permute-start.42 = (f32[3,18,1,128]{3,2,1,0:T(1,128)S(1)}, f32[3,18,1,128]{3,2,1,0:T(1,128)S(1)}, u32[]{:S(2)}, u32[]{:S(2)}) collective-permute-start(f32[3,18,1,128]{3,2,1,0:T(1,128)S(1)} %get-tuple-element.195), channel_id=1, source_target_pairs={{0,1},{1,2},{2,3},{3,4},{4,5},{5,6},{6,7},{7,8},{8,9},{9,10},{10,1... | collective-permute-start | bytes 82952 | tf_op jit(solution)/shard_map/ppermute | solution.py:41
  596.5 10.8 %collective-permute-start.43 = (f32[3,18,1,128]{3,2,1,0:T(1,128)S(1)}, f32[3,18,1,128]{3,2,1,0:T(1,128)S(1)}, u32[]{:S(2)}, u32[]{:S(2)}) collective-permute-start(f32[3,18,1,128]{3,2,1,0:T(1,128)S(1)} %get-tuple-element.196), channel_id=1, source_target_pairs={{1,0},{2,1},{3,2},{4,3},{5,4},{6,5},{7,6},{8,7},{9,8},{10,9},{11,1... | collective-permute-start | bytes 82952 | tf_op jit(solution)/shard_map/ppermute | solution.py:44
  601.9 42.0 %collective-permute-start.52 = (f32[4,1024]{1,0:T(4,128)S(1)}, f32[4,1024]{1,0:T(4,128)S(1)}, u32[]{:S(2)}, u32[]{:S(2)}) collective-permute-start(f32[4,1024]{1,0:T(4,128)S(1)} %get-tuple-element.291), channel_id=1, source_target_pairs={{0,1},{1,2},{2,3},{3,4},{4,5},{5,6},{6,7},{7,8},{8,9},{9,10},{10,1... | collective-permute-start | bytes 49160 | tf_op jit(solution)/shard_map/ppermute | solution.py:41
  602.0 45.5 %collective-permute-start.53 = (f32[4,1024]{1,0:T(4,128)S(1)}, f32[4,1024]{1,0:T(4,128)S(1)}, u32[]{:S(2)}, u32[]{:S(2)}) collective-permute-start(f32[4,1024]{1,0:T(4,128)S(1)} %get-tuple-element.292), channel_id=1, source_target_pairs={{1,0},{2,1},{3,2},{4,3},{5,4},{6,5},{7,6},{8,7},{9,8},{10,9},{11,1... | collective-permute-start | bytes 49160 | tf_op jit(solution)/shard_map/ppermute | solution.py:44
  664.3 118.2 %collective-permute-start.50 = (f32[3,18,1,128]{3,2,1,0:T(1,128)S(1)}, f32[3,18,1,128]{3,2,1,0:T(1,128)S(1)}, u32[]{:S(2)}, u32[]{:S(2)}) collective-permute-start(f32[3,18,1,128]{3,2,1,0:T(1,128)S(1)} %get-tuple-element.193), channel_id=1, source_target_pairs={{0,1},{1,2},{2,3},{3,4},{4,5},{5,6},{6,7},{7,8},{8,9},{9,10},{10,1... | collective-permute-start | bytes 82952 | tf_op jit(solution)/shard_map/ppermute | solution.py:41
  664.4 118.1 %collective-permute-start.51 = (f32[3,18,1,128]{3,2,1,0:T(1,128)S(1)}, f32[3,18,1,128]{3,2,1,0:T(1,128)S(1)}, u32[]{:S(2)}, u32[]{:S(2)}) collective-permute-start(f32[3,18,1,128]{3,2,1,0:T(1,128)S(1)} %get-tuple-element.194), channel_id=1, source_target_pairs={{1,0},{2,1},{3,2},{4,3},{5,4},{6,5},{7,6},{8,7},{9,8},{10,9},{11,1... | collective-permute-start | bytes 82952 | tf_op jit(solution)/shard_map/ppermute | solution.py:44
  (80 other events, 579.5 us)
